TPU v7x, 512 devices: a whole 4x4x16 slice. The times are simulated.
512 devices in a mesh: row: 16 (over z), col: 32 (over y, x, core).
Axes of the slice: x: 4, y: 4, z: 16, core: 2. Of those that a mesh axis runs over, the one named last changes fastest.
Arguments:
- new_keys: bfloat16 [1024, 28672], P('col', 'row'), may hold values from -6 to 6
- precision: bfloat16 [28672, 28672], P('row', 'col'), may hold values from -0.03125 to 0.03125
- stored_keys: bfloat16 [32, 256, 28672], P('row', None, 'col'), may hold values from -0.03125 to 0.03125
- pair_batch: int32 [16, 24], replicated, may hold values from 0 to 31, as said below
- pair_count: int32 [16], replicated, may hold values from 8 to 24, as said below
- batch_length: int32 [32], replicated, may hold values from 64 to 256
- batch_slot: int32 [32], replicated, may hold values from 0 to 31, each once
Outputs:
- whitened: bfloat16 [1024, 28672], P('row', 'col')
- intersections: float32 [16, 24, 64, 256], P('row', None, 'col')
Inputs may be any that keep to these rules, and one draw needn't show every extreme that they name: `pair_batch`: the ids in one block's row are distinct; ids at places at or beyond the block's count are ignored. `pair_count`: some block lists exactly 24 batches. `batch_slot`: every store slot belongs to exactly one batch.
All inputs are finite; a program needn't handle non-finite values.
Results may differ from a plain program's by a relative error of at most 0.0029.
Values may be sent and summed in bfloat16 or wider, within the bound.
A program may use at most 64 MiB of HBM per device.

v0:
```python
import jax
import jax.numpy as jnp
from jax import lax
from jax.sharding import PartitionSpec as P


def shards(new_keys, precision, stored_keys, pair_batch, pair_count, batch_length, batch_slot):
    row_count = lax.axis_size("row")
    col_count = lax.axis_size("col")
    row_index = lax.axis_index("row")
    total_keys = new_keys.shape[0] * col_count
    block_keys = total_keys // row_count
    part_keys = block_keys // col_count
    local_batches, batch_keys, width = stored_keys.shape
    partial_value = jnp.dot(
        lax.all_gather(new_keys, "col", axis=0, tiled=True),
        precision,
        preferred_element_type=jnp.float32,
    )
    summed = lax.psum_scatter(partial_value, "row", scatter_dimension=0, tiled=True)
    whitened = summed.astype(jnp.bfloat16)
    every_row = lax.all_gather(whitened, "row", axis=0, tiled=True)
    rows = every_row.reshape(row_count, col_count, part_keys, width)
    terms = jnp.einsum("bcid,sjd->csbij", rows, stored_keys, preferred_element_type=jnp.float32)
    mine = lax.psum_scatter(terms, "col", scatter_dimension=0, tiled=True)[0]
    routed = lax.all_to_all(mine, "row", split_axis=1, concat_axis=0, tiled=True)
    table = routed[:, 0]
    listed = pair_batch[row_index]
    slots = batch_slot[listed]
    lengths = batch_length[listed]
    count = pair_count[row_index]
    picked = jnp.take(table, slots, axis=0)
    places = jnp.arange(slots.shape[0], dtype=jnp.int32)
    columns = jnp.arange(batch_keys, dtype=jnp.int32)
    keep = (places < count)[:, None, None] & (columns[None, None, :] < lengths[:, None, None])
    shares = jnp.where(keep, picked, jnp.zeros_like(picked))
    return (whitened, shares[None])


def solution(mesh):
    placed = (P("col", "row"), P("row", "col"), P("row", None, "col"), P(), P(), P(), P())
    return jax.shard_map(
        shards,
        mesh=mesh,
        in_specs=placed,
        out_specs=(P("row", "col"), P("row", None, "col", None)),
        check_vma=False,
    )
```

profile of v0, /device:TPU:6, one launch (start us, length us, event | category | flops | bytes accessed | tf_op | source)
XLA Modules:
  0.0 379.6 jit_solution(4652722605744629083)
XLA Ops:
  7.2 0.0 copy-start
  7.2 0.0 all-gather.3.cloned.1.call-start
  7.2 0.7 all-gather.3.cloned.1.call-update
  7.9 0.0 reduce-scatter.3.cloned.1.call-start
  8.0 68.1 %all-gather.3.cloned.1.call-done = bf16[1024,1792]{1,0:T(8,128)(2,1)} async-done(((bf16[32,1792]{1,0:T(8,128)(2,1)}), bf16[1024,1792]{1,0:T(8,128)(2,1)}) %all-gather.3.cloned.1.call-update) | async-done | bytes 3670032 | tf_op jit(solution)/shard_map/all_gather | solution.py:16
  76.0 7.8 %fusion.10 = f32[1024,896]{1,0:T(8,128)} fusion(bf16[1024,1792]{1,0:T(8,128)(2,1)} %all-gather.3.cloned.1.call-done, bf16[1792,896]{1,0:T(8,128)(2,1)S(1)} %copy-done), kind=kOutput, calls=%fused_computation.20 | convolution fusion | flops 3288334336 | bytes 10551296 | tf_op jit(solution)/shard_map/dot_general | solution.py:15
  83.8 0.0 reduce-scatter.3.cloned.1.call-update
  83.8 0.0 all-gather.5.cloned.1.call-start
  83.9 78.2 %reduce-scatter.3.cloned.1.call-done = f32[64,896]{1,0:T(8,128)} async-done(((f32[1024,896]{1,0:T(8,128)}), f32[64,896]{1,0:T(8,128)}) %reduce-scatter.3.cloned.1.call-update) | async-done | bytes 229392 | tf_op jit(solution)/shard_map/reduce_scatter | solution.py:20
  162.1 1.6 convert_element_type.3
  163.7 0.0 all-gather.5.cloned.1.call-update
  163.7 0.0 reduce-scatter.5.cloned.1.call-start
  163.8 72.0 %all-gather.5.cloned.1.call-done = bf16[1024,896]{1,0:T(8,128)(2,1)} async-done(((bf16[64,896]{1,0:T(8,128)(2,1)}), bf16[1024,896]{1,0:T(8,128)(2,1)}) %all-gather.5.cloned.1.call-update) | async-done | bytes 1835024 | tf_op jit(solution)/shard_map/all_gather | solution.py:22
  235.8 4.8 %reshape.105 = bf16[16,32,2,896]{3,2,1,0:T(2,128)(2,1)} reshape(bf16[1024,896]{1,0:T(8,128)(2,1)} %all-gather.5.cloned.1.call-done) | data formatting | bytes 3670016 | tf_op jit(solution)/shard_map/reshape | solution.py:23
  240.7 3.0 fusion.2
  243.7 0.0 copy-start.3
  243.7 0.0 copy-start.1
  243.7 0.0 copy-start.2
  243.7 2.5 copy.16
  246.2 0.0 reduce-scatter.5.cloned.1.call-update
  246.3 0.6 dynamic_slice.6
  246.9 0.7 fusion.8
  247.6 0.7 gather_fusion.1
  248.3 96.7 %reduce-scatter.5.cloned.1.call-done = f32[1,2,16,2,256]{4,2,3,1,0:T(8,128)} async-done(((f32[32,2,16,2,256]{4,2,3,1,0:T(8,128)}), f32[1,2,16,2,256]{4,2,3,1,0:T(8,128)}) %reduce-scatter.5.cloned.1.call-update) | async-done | bytes 65552 | tf_op jit(solution)/shard_map/reduce_scatter | solution.py:25
  345.1 1.5 copy.17
  346.6 12.3 %all-to-all-start = ((f32[2,16,2,256]{3,2,0,1:T(2,128)}), f32[2,16,2,256]{3,2,0,1:T(2,128)S(1)}, u32[]{:S(2)}, u32[]{:S(2)}) async-start(f32[2,16,2,256]{3,2,0,1:T(2,128)} %copy.17), calls=%async_computation.2 | async-start | bytes 131072 | tf_op jit(solution)/shard_map/all_to_all | solution.py:26
  358.9 0.7 iota_compare_fusion.1
  359.6 0.7 gather_fusion
  360.3 0.1 fusion.7
  360.4 11.4 %all-to-all-done = f32[2,16,2,256]{3,2,0,1:T(2,128)S(1)} async-done(((f32[2,16,2,256]{3,2,0,1:T(2,128)}), f32[2,16,2,256]{3,2,0,1:T(2,128)S(1)}, u32[]{:S(2)}, u32[]{:S(2)}) %all-to-all-start) | async-done | bytes 65568 | tf_op jit(solution)/shard_map/all_to_all | solution.py:26
  371.8 0.6 gather_fusion.2
  372.4 0.7 fusion.6
  (8 shorter events, 0.0 us)
Async XLA Ops:
  7.2 68.9 %copy-start = (bf16[1792,896]{1,0:T(8,128)(2,1)S(1)}, bf16[1792,896]{1,0:T(8,128)(2,1)}, u32[]{:S(2)}) copy-start(bf16[1792,896]{1,0:T(8,128)(2,1)} %param.8) | copy-start | bytes 9633796
  7.2 68.9 %all-gather.3.cloned.1.call-start = ((), (), s32[]{:S(2)}) async-start(), calls=%async_computation.3 | async-start | bytes 3784704 | tf_op jit(solution)/shard_map/all_gather | solution.py:16
  7.9 154.2 %reduce-scatter.3.cloned.1.call-start = ((), (), s32[]{:S(2)}) async-start(), calls=%async_computation.4 | async-start | bytes 3899392 | tf_op jit(solution)/shard_map/reduce_scatter | solution.py:20
  83.8 152.0 %all-gather.5.cloned.1.call-start = ((), (), s32[]{:S(2)}) async-start(), calls=%async_computation.5 | async-start | bytes 1949696 | tf_op jit(solution)/shard_map/all_gather | solution.py:22
  163.7 181.3 %reduce-scatter.5.cloned.1.call-start = ((), (), s32[]{:S(2)}) async-start(), calls=%async_computation.6 | async-start | bytes 2162688 | tf_op jit(solution)/shard_map/reduce_scatter | solution.py:25
  243.7 2.6 copy-start.3
  243.7 3.9 %copy-start.1 = (s32[32]{0:T(128)S(1)}, s32[32]{0:T(128)}, u32[]{:S(2)}) copy-start(s32[32]{0:T(128)} %param.13) | copy-start | bytes 388
  243.7 115.9 %copy-start.2 = (s32[32]{0:T(128)S(1)}, s32[32]{0:T(128)}, u32[]{:S(2)}) copy-start(s32[32]{0:T(128)} %param.12) | copy-start | bytes 388
  346.6 25.2 %all-to-all-start = ((f32[2,16,2,256]{3,2,0,1:T(2,128)}), f32[2,16,2,256]{3,2,0,1:T(2,128)S(1)}, u32[]{:S(2)}, u32[]{:S(2)}) async-start(f32[2,16,2,256]{3,2,0,1:T(2,128)} %copy.17), calls=%async_computation.2 | async-start | bytes 131072 | tf_op jit(solution)/shard_map/all_to_all | solution.py:26
Sparse Core Ops, SparseCore 0:
  11.1 64.8 all-gather.2
  84.0 78.1 reduce-scatter.2
  164.8 71.0 all-gather.4
  246.4 98.6 reduce-scatter.4
where the time goes:
time: 380 us
  waiting for transfers between devices  327 us (86%)
  between operations  13.9 us (4%)
  starting transfers between devices  12.5 us (3%)
  local copies, waits for them, and re-layouts  11.5 us (3%)
  matrix products  10.8 us (3%)
    reduce_scatter x1, waiting for transfers between devices, shards(): mine = lax.psum_scatter(terms, 'col', scatter_dimension=0, tiled=True)[0]  96.7 us
    reduce_scatter x1, waiting for transfers between devices, shards(): lax.psum_scatter(partial_value, 'row', scatter_dimension=0, tiled=True)  78.2 us
    all_gather x1, waiting for transfers between devices, shards(): every_row = lax.all_gather(whitened, 'row', axis=0, tiled=True)  72 us
    all_gather x1, waiting for transfers between devices, shards(): lax.all_gather(new_keys, 'col', axis=0, tiled=True)  68.1 us
    all_to_all x1, starting transfers between devices, shards(): lax.all_to_all(mine, 'row', split_axis=1, concat_axis=0, tiled=True)  12.3 us
    all_to_all x1, waiting for transfers between devices, shards(): lax.all_to_all(mine, 'row', split_axis=1, concat_axis=0, tiled=True)  11.4 us
    dot_general x1, matrix products, shards(): jnp.dot(lax.all_gather(new_keys, 'col', axis=0, tiled=True), precision, p...  7.77 us
  transfers between devices with their start and end apart: 5, of which 5 were waited for; matrix products, arithmetic and copies ran while one was open for 1% of the time, Pallas kernels for 0%

commit v1 on v0

--- a/solution.py
+++ b/solution.py
@@ -13,7 +13,10 @@
     part_keys = block_keys // col_count
     local_batches, batch_keys, width = stored_keys.shape
     partial_value = jnp.dot(
-        lax.all_gather(new_keys, "col", axis=0, tiled=True),
+        jnp.concatenate(
+            jax.lax.all_to_all(jnp.stack([new_keys] * jax.lax.axis_size("col")), "col", 0, 0),
+            axis=0,
+        ),
         precision,
         preferred_element_type=jnp.float32,
     )

time: 380 us -> 364 us (0.958)
  waiting for transfers between devices: 327 us -> 260 us
  blocking collectives: 0 us -> 51.7 us
    all_gather x1 -> x0, waiting for transfers between devices: 68.1 us -> none  [shards(): lax.all_gather(new_keys, 'col', axis=0, tiled=True)]
    all_to_all x0 -> x1, blocking collectives: none -> 51.7 us  [shards(): jax.lax.all_to_all(jnp.stack([new_keys] * jax.lax.axis_size('col')), 'col...]
  transfers between devices with their start and end apart: 5 -> 4, of which waited for: 5 -> 4; matrix products, arithmetic and copies ran while one was open for 1% -> 1% of each run, Pallas kernels for 0% -> 0%
where the time goes in v1:
time: 364 us
  waiting for transfers between devices  260 us (71%)
  blocking collectives  51.7 us (14%)
  between operations  13.8 us (4%)
  local copies, waits for them, and re-layouts  12.9 us (4%)
  starting transfers between devices  12.4 us (3%)
  matrix products  8.78 us (2%)
  other arithmetic  3.77 us (1%)
    reduce_scatter x1, waiting for transfers between devices, shards(): mine = lax.psum_scatter(terms, 'col', scatter_dimension=0, tiled=True)[0]  96.7 us
    reduce_scatter x1, waiting for transfers between devices, shards(): lax.psum_scatter(partial_value, 'row', scatter_dimension=0, tiled=True)  80.5 us
    all_gather x1, waiting for transfers between devices, shards(): every_row = lax.all_gather(whitened, 'row', axis=0, tiled=True)  71.4 us
    all_to_all x1, blocking collectives, shards(): jax.lax.all_to_all(jnp.stack([new_keys] * jax.lax.axis_size('col')), 'col...  51.7 us
    all_to_all x1, starting transfers between devices, shards(): lax.all_to_all(mine, 'row', split_axis=1, concat_axis=0, tiled=True)  12.3 us
    all_to_all x1, waiting for transfers between devices, shards(): lax.all_to_all(mine, 'row', split_axis=1, concat_axis=0, tiled=True)  11.4 us
  transfers between devices with their start and end apart: 4, of which 4 were waited for; matrix products, arithmetic and copies ran while one was open for 1% of the time, Pallas kernels for 0%

profile of v1, /device:TPU:6, one launch (start us, length us, event | category | flops | bytes accessed | tf_op | source)
XLA Modules:
  0.0 363.5 jit_solution(14834331706619527535)
XLA Ops:
  7.2 0.0 copy-start
  7.2 0.0 reduce-scatter.3.cloned.1.call-start
  7.2 1.5 stack.2
  8.7 51.7 %all_to_all.20 = bf16[32,32,1792]{2,1,0:T(8,128)(2,1)S(1)} all-to-all(bf16[32,32,1792]{2,1,0:T(8,128)(2,1)S(1)} %stack.2), channel_id=1, replica_groups=mesh['row'=16,'col'=32] {'col'}, dimensions={0} | all-to-all | bytes 7340032 | tf_op jit(solution)/shard_map/all_to_all | solution.py:17
  60.4 0.0 copy-done
  60.4 5.8 %fusion.10 = f32[1024,896]{1,0:T(8,128)} fusion(bf16[1024,1792]{1,0:T(8,128)(2,1)S(1)} %bitcast.30, bf16[1792,896]{1,0:T(8,128)(2,1)S(1)} %copy-done), kind=kOutput, calls=%fused_computation.20 | convolution fusion | flops 3288334336 | bytes 10551296 | tf_op jit(solution)/shard_map/dot_general | solution.py:15
  66.2 0.0 reduce-scatter.3.cloned.1.call-update
  66.2 0.0 all-gather.2.cloned.1.call-start
  66.2 80.5 %reduce-scatter.3.cloned.1.call-done = f32[64,896]{1,0:T(8,128)} async-done(((f32[1024,896]{1,0:T(8,128)}), f32[64,896]{1,0:T(8,128)}) %reduce-scatter.3.cloned.1.call-update) | async-done | bytes 229392 | tf_op jit(solution)/shard_map/reduce_scatter | solution.py:23
  146.7 1.6 convert_element_type.3
  148.3 0.0 all-gather.2.cloned.1.call-update
  148.3 0.0 reduce-scatter.5.cloned.1.call-start
  148.4 71.4 %all-gather.2.cloned.1.call-done = bf16[1024,896]{1,0:T(8,128)(2,1)} async-done(((bf16[64,896]{1,0:T(8,128)(2,1)}), bf16[1024,896]{1,0:T(8,128)(2,1)}) %all-gather.2.cloned.1.call-update) | async-done | bytes 1835024 | tf_op jit(solution)/shard_map/all_gather | solution.py:25
  219.8 4.8 %reshape.111 = bf16[16,32,2,896]{3,2,1,0:T(2,128)(2,1)} reshape(bf16[1024,896]{1,0:T(8,128)(2,1)} %all-gather.2.cloned.1.call-done) | data formatting | bytes 3670016 | tf_op jit(solution)/shard_map/reshape | solution.py:26
  224.5 3.0 fusion.2
  227.6 0.0 copy-start.3
  227.6 0.0 copy-start.1
  227.6 0.0 copy-start.2
  227.6 2.6 copy.16
  230.1 0.0 reduce-scatter.5.cloned.1.call-update
  230.2 0.6 dynamic_slice.6
  230.8 0.7 fusion.8
  231.5 0.7 gather_fusion.1
  232.2 96.7 %reduce-scatter.5.cloned.1.call-done = f32[1,2,16,2,256]{4,2,3,1,0:T(8,128)} async-done(((f32[32,2,16,2,256]{4,2,3,1,0:T(8,128)}), f32[1,2,16,2,256]{4,2,3,1,0:T(8,128)}) %reduce-scatter.5.cloned.1.call-update) | async-done | bytes 65552 | tf_op jit(solution)/shard_map/reduce_scatter | solution.py:28
  329.0 1.5 copy.17
  330.5 12.3 %all-to-all-start.1 = ((f32[2,16,2,256]{3,2,0,1:T(2,128)}), f32[2,16,2,256]{3,2,0,1:T(2,128)S(1)}, u32[]{:S(2)}, u32[]{:S(2)}) async-start(f32[2,16,2,256]{3,2,0,1:T(2,128)} %copy.17), calls=%async_computation.3 | async-start | bytes 131072 | tf_op jit(solution)/shard_map/all_to_all | solution.py:29
  342.8 0.7 iota_compare_fusion.1
  343.5 0.7 gather_fusion
  344.2 0.1 fusion.7
  344.2 11.4 %all-to-all-done.1 = f32[2,16,2,256]{3,2,0,1:T(2,128)S(1)} async-done(((f32[2,16,2,256]{3,2,0,1:T(2,128)}), f32[2,16,2,256]{3,2,0,1:T(2,128)S(1)}, u32[]{:S(2)}, u32[]{:S(2)}) %all-to-all-start.1) | async-done | bytes 65568 | tf_op jit(solution)/shard_map/all_to_all | solution.py:29
  355.7 0.6 gather_fusion.2
  356.3 0.7 fusion.6
  (7 shorter events, 0.0 us)
Async XLA Ops:
  7.2 53.2 %copy-start = (bf16[1792,896]{1,0:T(8,128)(2,1)S(1)}, bf16[1792,896]{1,0:T(8,128)(2,1)}, u32[]{:S(2)}) copy-start(bf16[1792,896]{1,0:T(8,128)(2,1)} %param.8) | copy-start | bytes 9633796
  7.2 139.5 %reduce-scatter.3.cloned.1.call-start = ((), (), s32[]{:S(2)}) async-start(), calls=%async_computation.4 | async-start | bytes 3899392 | tf_op jit(solution)/shard_map/reduce_scatter | solution.py:23
  66.2 153.6 %all-gather.2.cloned.1.call-start = ((), (), s32[]{:S(2)}) async-start(), calls=%async_computation.5 | async-start | bytes 1949696 | tf_op jit(solution)/shard_map/all_gather | solution.py:25
  148.3 180.6 %reduce-scatter.5.cloned.1.call-start = ((), (), s32[]{:S(2)}) async-start(), calls=%async_computation.6 | async-start | bytes 2162688 | tf_op jit(solution)/shard_map/reduce_scatter | solution.py:28
  227.6 2.6 copy-start.3
  227.6 3.9 %copy-start.1 = (s32[32]{0:T(128)S(1)}, s32[32]{0:T(128)}, u32[]{:S(2)}) copy-start(s32[32]{0:T(128)} %param.13) | copy-start | bytes 388
  227.6 115.9 %copy-start.2 = (s32[32]{0:T(128)S(1)}, s32[32]{0:T(128)}, u32[]{:S(2)}) copy-start(s32[32]{0:T(128)} %param.12) | copy-start | bytes 388
  330.5 25.2 %all-to-all-start.1 = ((f32[2,16,2,256]{3,2,0,1:T(2,128)}), f32[2,16,2,256]{3,2,0,1:T(2,128)S(1)}, u32[]{:S(2)}, u32[]{:S(2)}) async-start(f32[2,16,2,256]{3,2,0,1:T(2,128)} %copy.17), calls=%async_computation.3 | async-start | bytes 131072 | tf_op jit(solution)/shard_map/all_to_all | solution.py:29
Sparse Core Ops, SparseCore 0:
  66.3 80.3 reduce-scatter.2
  149.4 70.3 all-gather.1
  230.3 98.6 reduce-scatter.4
